TPU v7x, 32 devices: a whole 2x2x4 slice. The times are simulated.
32 devices in a mesh: section: 2 (over x), dp: 4 (over y, core), tensor: 4 (over z).
Axes of the slice: x: 2, y: 2, z: 4, core: 2. Of those that a mesh axis runs over, the one named last changes fastest.
Arguments:
- tokens: bfloat16 [8, 704, 768], P('dp', 'tensor'), may hold values from -6 to 6
- segment_ids: int32 [8, 704], P('dp'), may hold values from 0 to 3, as said below
- cotangent: bfloat16 [8, 704, 768], P('dp', 'tensor'), may hold values from -6 to 6
- norm_gain1: float32 [2, 768], P('section'), may hold values from 0.5 to 1.5
- w_in: bfloat16 [2, 768, 3, 768], P('section', None, None, 'tensor'), may hold values from -0.21875 to 0.21875
- short_taps: float32 [2, 3, 3, 768], P('section', None, None, 'tensor'), may hold values from -4 to 4
- cond_taps: float32 [2, 3, 768], P('section', None, 'tensor'), may hold values from -4 to 4
- spectrum: float32 [2, 2, 705, 768], P('section', None, None, 'tensor'), may hold values from -6 to 6
- spectral_gain: float32 [2, 2, 768], P('section', None, 'tensor'), may hold values from 0.3 to 3
- w_out: bfloat16 [2, 768, 768], P('section', 'tensor'), may hold values from -0.4375 to 0.4375
- norm_gain2: float32 [2, 768], P('section'), may hold values from 0.5 to 1.5
- w_gate_up: bfloat16 [2, 768, 2, 3072], P('section', None, None, 'tensor'), may hold values from -0.21875 to 0.21875
- w_down: bfloat16 [2, 3072, 768], P('section', 'tensor'), may hold values from -0.15625 to 0.15625
Outputs:
- layer_out: float32 [2, 8, 704, 768], P('section', 'dp', 'tensor')
- grad_in: float32 [2, 8, 704, 768], P('section', 'dp', 'tensor')
- grad_norm_gain1: float32 [2, 768], P('section')
- grad_w_in: float32 [2, 768, 3, 768], P('section', None, None, 'tensor')
- grad_short_taps: float32 [2, 3, 3, 768], P('section', None, None, 'tensor')
- grad_cond_taps: float32 [2, 3, 768], P('section', None, 'tensor')
- grad_spectrum: float32 [2, 2, 705, 768], P('section', None, None, 'tensor')
- grad_spectral_gain: float32 [2, 2, 768], P('section', None, 'tensor')
- grad_w_out: float32 [2, 768, 768], P('section', 'tensor')
- grad_norm_gain2: float32 [2, 768], P('section')
- grad_w_gate_up: float32 [2, 768, 2, 3072], P('section', None, None, 'tensor')
- grad_w_down: float32 [2, 3072, 768], P('section', 'tensor')
Inputs may be any that keep to these rules, and one draw needn't show every extreme that they name: `segment_ids`: in each pack the ids never fall along the rows, and each of the 4 ids holds one or more rows.
All inputs are finite; a program needn't handle non-finite values.
Results may differ from a plain program's by a relative error of at most 0.022.
The roundings to bfloat16 on the way count: a program that leaves them out, or rounds other values in their place, can miss the bound.
Values may be sent and summed in bfloat16 or wider, within the bound.
No kernel may reach another device: no remote copies, remote signals or barrier semaphores. Data moves between devices by JAX's collectives and lax.ppermute only.
A program may use at most 192 MiB of HBM per device.

v0:
```python
from functools import partial
import math
import jax
import jax.numpy as jnp
from jax import lax
from jax.sharding import PartitionSpec as P

SEGS = 4
highest = lax.Precision.HIGHEST


def from_behind(shard, axis, by):
    peers = lax.axis_size(axis)
    pairs = [(i, i + by) for i in range(peers) if 0 <= i + by < peers]
    return lax.ppermute(shard, axis, pairs)


def layer_norm(values, gain):
    row_mean = jnp.mean(values, axis=-1, keepdims=True)
    centred = values - row_mean
    variance = jnp.mean(centred * centred, axis=-1, keepdims=True)
    return centred * lax.rsqrt(variance + 1e-05) * gain


def neighbours(segments):
    equal = (segments[1:] == segments[:-1]).astype(jnp.float32)
    blank = jnp.zeros((1,), jnp.float32)
    return (jnp.concatenate([blank, equal]), jnp.concatenate([equal, blank]))


def masked_short(values, taps, same_prev, same_next):
    blank = jnp.zeros((1, values.shape[1]), values.dtype)
    before = jnp.concatenate([blank, values[:-1]], axis=0) * same_prev[:, None]
    after = jnp.concatenate([values[1:], blank], axis=0) * same_next[:, None]
    return taps[0] * before + taps[1] * values + taps[2] * after


def spectral_tables(pack_len):
    period = 2 * pack_len
    freq_index = lax.broadcasted_iota(jnp.int32, (pack_len + 1, pack_len), 0)
    place_index = lax.broadcasted_iota(jnp.int32, (pack_len + 1, pack_len), 1)
    angle = (freq_index * place_index % period).astype(jnp.float32) * (2.0 * math.pi / period)
    cosine = jnp.cos(angle)
    sine = jnp.sin(angle)
    forward_table = jnp.concatenate([cosine, -sine], axis=0)
    freq_column = freq_index[:, :1]
    column_weight = jnp.where((freq_column == 0) | (freq_column == pack_len), 1.0, 2.0) / period
    inverse_table = jnp.concatenate([cosine * column_weight, -sine * column_weight], axis=0).T
    return (forward_table, inverse_table)


def orchid_mix(proj, short_taps, cond_taps, spectrum, spectral_gain, segments, tables):
    forward_table, inverse_table = tables
    pack_len = proj.shape[0]
    channels = proj.shape[1] // 3
    freqs = pack_len + 1
    same_prev, same_next = neighbours(segments)
    shorted = masked_short(proj, short_taps, same_prev, same_next)
    query = shorted[:, :channels]
    key_part = shorted[:, channels : 2 * channels]
    value_part = shorted[:, 2 * channels :]
    condition = masked_short(key_part, cond_taps, same_prev, same_next)
    cond_hat = jnp.dot(forward_table, condition, precision=highest)
    scale_in = spectral_gain[0] / math.sqrt(pack_len)
    filt_re = spectrum[0] + spectral_gain[1] * jnp.tanh(scale_in * cond_hat[:freqs])
    filt_im = spectrum[1] + spectral_gain[1] * jnp.tanh(scale_in * cond_hat[freqs:])
    masks = (segments[:, None] == jnp.arange(SEGS, dtype=jnp.int32)[None, :]).astype(jnp.float32)
    pieces = (masks[:, :, None] * value_part[:, None, :]).reshape(pack_len, SEGS * channels)
    piece_hat = jnp.dot(forward_table, pieces, precision=highest).reshape(2, freqs, SEGS, channels)
    real_part = piece_hat[0] * filt_re[:, None, :] - piece_hat[1] * filt_im[:, None, :]
    imag_part = piece_hat[0] * filt_im[:, None, :] + piece_hat[1] * filt_re[:, None, :]
    joined = jnp.concatenate([real_part, imag_part], axis=0).reshape(2 * freqs, SEGS * channels)
    conv = jnp.dot(inverse_table, joined, precision=highest).reshape(pack_len, SEGS, channels)
    mixed = jnp.sum(conv * masks[:, :, None], axis=1)
    return query * mixed


def glu_act(both_parts):
    half_width = both_parts.shape[1] // 2
    return jax.nn.silu(both_parts[:, :half_width]) * both_parts[:, half_width:]


def mixer_local(gathered, segments, params, tables):
    (
        gain_one,
        w_in,
        short_taps,
        cond_taps,
        spectrum,
        spectral_gain,
        w_out,
        gain_two,
        w_gate_up,
        w_down,
    ) = params
    proj = jnp.dot(gathered, w_in, preferred_element_type=jnp.float32)
    mixer = partial(orchid_mix, segments=segments, tables=tables)
    mixed, mix_pull = jax.vjp(mixer, proj, short_taps, cond_taps, spectrum, spectral_gain)
    return (mixed.astype(jnp.bfloat16), mix_pull)


def glu_local(gathered_two, w_gate_up):
    both_parts = jnp.dot(gathered_two, w_gate_up, preferred_element_type=jnp.float32)
    act, act_pull = jax.vjp(glu_act, both_parts)
    return (act.astype(jnp.bfloat16), act_pull)


def run_layer(layer_input, segments, params, tables, finish):
    (
        gain_one,
        w_in,
        short_taps,
        cond_taps,
        spectrum,
        spectral_gain,
        w_out,
        gain_two,
        w_gate_up,
        w_down,
    ) = params
    normed, norm_pull = jax.vjp(layer_norm, layer_input, gain_one)
    gathered = lax.all_gather(normed.astype(jnp.bfloat16), "tensor", axis=0, tiled=True)
    mixed_low, mix_pull = mixer_local(gathered, segments, params, tables)
    hidden = layer_input + lax.psum_scatter(
        jnp.dot(mixed_low, w_out, preferred_element_type=jnp.float32),
        "tensor",
        scatter_dimension=0,
        tiled=True,
    )
    normed_two, norm_pull_two = jax.vjp(layer_norm, hidden, gain_two)
    gathered_two = lax.all_gather(normed_two.astype(jnp.bfloat16), "tensor", axis=0, tiled=True)
    act_low, act_pull = glu_local(gathered_two, w_gate_up)
    saved = (
        norm_pull,
        gathered,
        mixed_low,
        mix_pull,
        norm_pull_two,
        gathered_two,
        act_pull,
        act_low,
    )
    front_rows = (gathered, hidden, gathered_two)
    if finish:
        return (
            hidden
            + lax.psum_scatter(
                jnp.dot(act_low, w_down, preferred_element_type=jnp.float32),
                "tensor",
                scatter_dimension=0,
                tiled=True,
            ),
            saved,
            front_rows,
        )
    return (hidden, saved, front_rows)


def back_layer(layer_input, segments, params, tables, grad_out):
    (
        gain_one,
        w_in,
        short_taps,
        cond_taps,
        spectrum,
        spectral_gain,
        w_out,
        gain_two,
        w_gate_up,
        w_down,
    ) = params
    hidden, saved, front_rows = run_layer(layer_input, segments, params, tables, False)
    norm_pull, gathered, mixed_low, mix_pull, norm_pull_two, gathered_two, act_pull, act_low = saved
    grad_rows = lax.all_gather(grad_out.astype(jnp.bfloat16), "tensor", axis=0, tiled=True)
    grad_act = jnp.einsum("ld,fd->lf", grad_rows, w_down, preferred_element_type=jnp.float32)
    grad_down = jnp.einsum("lf,ld->fd", act_low, grad_rows, preferred_element_type=jnp.float32)
    grad_both = act_pull(grad_act)[0].astype(jnp.bfloat16)
    grad_gate_up = jnp.einsum(
        "ld,lf->df", gathered_two, grad_both, preferred_element_type=jnp.float32
    )
    piece = grad_both
    grad_normed_two = lax.psum_scatter(
        jnp.einsum("lf,df->ld", piece, w_gate_up, preferred_element_type=jnp.float32),
        "tensor",
        scatter_dimension=0,
        tiled=True,
    )
    grad_hidden_part, grad_gain_two = norm_pull_two(grad_normed_two)
    grad_hidden = grad_out + grad_hidden_part
    grad_mix_rows = lax.all_gather(grad_hidden.astype(jnp.bfloat16), "tensor", axis=0, tiled=True)
    grad_mixed = jnp.einsum("ld,cd->lc", grad_mix_rows, w_out, preferred_element_type=jnp.float32)
    grad_w_out = jnp.einsum(
        "lc,ld->cd", mixed_low, grad_mix_rows, preferred_element_type=jnp.float32
    )
    grad_proj, grad_short, grad_cond, grad_spectrum, grad_spectral = mix_pull(grad_mixed)
    grad_proj_low = grad_proj.astype(jnp.bfloat16)
    grad_w_in = jnp.einsum("ld,lc->dc", gathered, grad_proj_low, preferred_element_type=jnp.float32)
    piece = grad_proj_low
    grad_normed = lax.psum_scatter(
        jnp.einsum("lc,dc->ld", piece, w_in, preferred_element_type=jnp.float32),
        "tensor",
        scatter_dimension=0,
        tiled=True,
    )
    grad_input_part, grad_gain_one = norm_pull(grad_normed)
    grad_input = grad_hidden + grad_input_part
    weight_terms = (
        grad_w_in,
        grad_short,
        grad_cond,
        grad_spectrum,
        grad_spectral,
        grad_w_out,
        grad_gate_up,
        grad_down,
    )
    return (grad_input, (grad_gain_one, grad_gain_two), weight_terms)


def per_device(
    tokens,
    segment_ids,
    cotangent,
    norm_gain1,
    w_in,
    short_taps,
    cond_taps,
    spectrum,
    spectral_gain,
    w_out,
    norm_gain2,
    w_gate_up,
    w_down,
):
    pack_count, row_count, model_width = tokens.shape
    pack_len = segment_ids.shape[1]
    channels = w_in.shape[3]
    hidden_cols = w_gate_up.shape[3]
    params = (
        norm_gain1[0],
        w_in[0].reshape(model_width, 3 * channels),
        short_taps[0].reshape(3, 3 * channels),
        cond_taps[0],
        spectrum[0],
        spectral_gain[0],
        w_out[0],
        norm_gain2[0],
        w_gate_up[0].reshape(model_width, 2 * hidden_cols),
        w_down[0],
    )
    tables = spectral_tables(pack_len)
    section_index = lax.axis_index("section")
    last_section = lax.axis_size("section") - 1
    step_count = pack_count + last_section

    def forward_step(loop_state, step_index):
        sent, kept_in, kept_out, kept_extra = loop_state
        received = from_behind(sent, "section", 1)
        micro = step_index - section_index
        is_valid = (micro >= 0) & (micro < pack_count)
        slot_index = jnp.clip(micro, 0, pack_count - 1)
        own_rows = lax.dynamic_index_in_dim(tokens, slot_index, 0, keepdims=False).astype(
            jnp.float32
        )
        layer_input = jnp.where(section_index == 0, own_rows, received)
        segments = lax.dynamic_index_in_dim(segment_ids, slot_index, 0, keepdims=False)
        result, unused_saved, front_rows = run_layer(layer_input, segments, params, tables, True)
        kept_in = jnp.where(
            is_valid, lax.dynamic_update_index_in_dim(kept_in, layer_input, slot_index, 0), kept_in
        )
        kept_out = jnp.where(
            is_valid, lax.dynamic_update_index_in_dim(kept_out, result, slot_index, 0), kept_out
        )
        return ((result, kept_in, kept_out, kept_extra), None)

    extra_start = ()
    start_state = (
        jnp.zeros((row_count, model_width), jnp.float32),
        jnp.zeros((pack_count, row_count, model_width), jnp.float32),
        jnp.zeros((pack_count, row_count, model_width), jnp.float32),
        extra_start,
    )
    (unused_rows, kept_in, kept_out, kept_extra), unused_steps = lax.scan(
        forward_step, start_state, jnp.arange(step_count)
    )
    weight_shapes = (
        params[1],
        params[2],
        params[3],
        params[4],
        params[5],
        params[6],
        params[8],
        params[9],
    )
    zero_weights = tuple((jnp.zeros(array.shape, jnp.float32) for array in weight_shapes))
    zero_gains = (jnp.zeros((model_width,), jnp.float32), jnp.zeros((model_width,), jnp.float32))

    def backward_step(loop_state, step_index):
        sent, kept_grad, gain_totals, weight_totals = loop_state
        received = from_behind(sent, "section", -1)
        micro = step_index - (last_section - section_index)
        is_valid = (micro >= 0) & (micro < pack_count)
        slot_index = jnp.clip(micro, 0, pack_count - 1)
        own_grad = lax.dynamic_index_in_dim(cotangent, slot_index, 0, keepdims=False).astype(
            jnp.float32
        )
        grad_out = jnp.where(section_index == last_section, own_grad, received)
        layer_input = lax.dynamic_index_in_dim(kept_in, slot_index, 0, keepdims=False)
        segments = lax.dynamic_index_in_dim(segment_ids, slot_index, 0, keepdims=False)
        grad_input, gain_terms, weight_terms = back_layer(
            layer_input, segments, params, tables, grad_out
        )
        gain_terms = tuple((jnp.where(is_valid, term, 0.0) for term in gain_terms))
        term_in, term_short, term_cond, term_spec, term_gain, term_out, term_gate_up, term_down = (
            tuple((jnp.where(is_valid, term, 0.0) for term in weight_terms))
        )
        new_terms = (
            term_in,
            term_short,
            term_cond,
            term_spec,
            term_gain,
            term_out,
            term_gate_up,
            term_down,
        )
        weight_totals = tuple((total + term for total, term in zip(weight_totals, new_terms)))
        gain_totals = tuple((total + term for total, term in zip(gain_totals, gain_terms)))
        kept_grad = jnp.where(
            is_valid,
            lax.dynamic_update_index_in_dim(kept_grad, grad_input, slot_index, 0),
            kept_grad,
        )
        return ((grad_input, kept_grad, gain_totals, weight_totals), None)

    back_start = (
        jnp.zeros((row_count, model_width), jnp.float32),
        jnp.zeros((pack_count, row_count, model_width), jnp.float32),
        zero_gains,
        zero_weights,
    )
    (unused_grad, kept_grad, gain_totals, weight_totals), unused_back = lax.scan(
        backward_step, back_start, jnp.arange(step_count)
    )
    sum_in, sum_short, sum_cond, sum_spec, sum_gain, sum_out, sum_gate_up, sum_down = weight_totals
    sum_in, sum_short, sum_cond, sum_spec, sum_gain, sum_out, sum_gate_up, sum_down = lax.psum(
        (sum_in, sum_short, sum_cond, sum_spec, sum_gain, sum_out, sum_gate_up, sum_down), "dp"
    )
    gain_first, gain_second = gain_totals
    gain_first, gain_second = lax.psum((gain_first, gain_second), ("dp", "tensor"))
    return (
        kept_out[None],
        kept_grad[None],
        gain_first[None],
        sum_in.reshape(1, model_width, 3, channels),
        sum_short.reshape(1, 3, 3, channels),
        sum_cond[None],
        sum_spec[None],
        sum_gain[None],
        sum_out[None],
        gain_second[None],
        sum_gate_up.reshape(1, model_width, 2, hidden_cols),
        sum_down[None],
    )


def solution(mesh):
    return jax.shard_map(
        per_device,
        mesh=mesh,
        in_specs=(
            P("dp", "tensor", None),
            P("dp", None),
            P("dp", "tensor", None),
            P("section", None),
            P("section", None, None, "tensor"),
            P("section", None, None, "tensor"),
            P("section", None, "tensor"),
            P("section", None, None, "tensor"),
            P("section", None, "tensor"),
            P("section", "tensor", None),
            P("section", None),
            P("section", None, None, "tensor"),
            P("section", "tensor", None),
        ),
        out_specs=(
            P("section", "dp", "tensor", None),
            P("section", "dp", "tensor", None),
            P("section", None),
            P("section", None, None, "tensor"),
            P("section", None, None, "tensor"),
            P("section", None, "tensor"),
            P("section", None, None, "tensor"),
            P("section", None, "tensor"),
            P("section", "tensor", None),
            P("section", None),
            P("section", None, None, "tensor"),
            P("section", "tensor", None),
        ),
        check_vma=False,
    )
```

profile of v0, /device:TPU:0, one launch (start us, length us, event | category | flops | bytes accessed | tf_op | source)
XLA Modules:
  0.0 2237.0 jit_solution(2906031752056489237)
XLA Ops:
  48.2 704.4 %while.51 = (s32[]{:T(128)}, f32[176,768]{1,0:T(8,128)S(1)}, f32[2,176,768]{2,1,0:T(8,128)S(1)}, f32[2,176,768]{2,1,0:T(8,128)}, pred[]{:T(512)}, /*index=5*/s32...) while((s32[]{:T(128)}, f32[176,768]{1,0:T(8,128)S(1)}, ...), condition=%wide.region_8.9_spmd.clone, body=%wide.region_0.8_spmd.clone.sunk | while | flops 23922319360 | bytes 190306960 | solution.py:283
  67.5 30.6 %all-gather.7.cloned.1.call-done = bf16[704,768]{1,0:T(8,128)(2,1)} async-done(((bf16[176,768]{1,0:T(8,128)(2,1)}), bf16[704,768]{1,0:T(8,128)(2,1)}) %all-gather.7.cloned.1.call-update) | async-done | bytes 1081360 | tf_op jit(solution)/shard_map/while/body/eval_jaxpr/all_gather | solution.py:122
  113.5 13.8 convolution_bitcast_fusion.15
  136.2 13.8 fusion.255
  157.9 43.8 %reduce-scatter.6.cloned.1.call-done = f32[176,768]{1,0:T(8,128)} async-done(((f32[704,768]{1,0:T(8,128)}), f32[176,768]{1,0:T(8,128)}) %reduce-scatter.6.cloned.1.call-update) | async-done | bytes 540688 | tf_op jit(solution)/shard_map/while/body/eval_jaxpr/reduce_scatter | solution.py:124
  204.0 28.0 %all-gather.9.cloned.1.call-done = bf16[704,768]{1,0:T(8,128)(2,1)} async-done(((bf16[176,768]{1,0:T(8,128)(2,1)}), bf16[704,768]{1,0:T(8,128)(2,1)}) %all-gather.9.cloned.1.call-update) | async-done | bytes 1081360 | tf_op jit(solution)/shard_map/while/body/eval_jaxpr/all_gather | solution.py:131
  238.6 44.6 %reduce-scatter.8.cloned.1.call-done = f32[176,768]{1,0:T(8,128)} async-done(((f32[704,768]{1,0:T(8,128)}), f32[176,768]{1,0:T(8,128)}) %reduce-scatter.8.cloned.1.call-update) | async-done | bytes 540688 | tf_op jit(solution)/shard_map/while/body/eval_jaxpr/reduce_scatter | solution.py:147
  302.8 28.9 %all-gather.7.cloned.1.call-done = bf16[704,768]{1,0:T(8,128)(2,1)} async-done(((bf16[176,768]{1,0:T(8,128)(2,1)}), bf16[704,768]{1,0:T(8,128)(2,1)}) %all-gather.7.cloned.1.call-update) | async-done | bytes 1081360 | tf_op jit(solution)/shard_map/while/body/eval_jaxpr/all_gather | solution.py:122
  347.1 13.8 convolution_bitcast_fusion.15
  369.8 13.8 fusion.255
  391.5 43.8 %reduce-scatter.6.cloned.1.call-done = f32[176,768]{1,0:T(8,128)} async-done(((f32[704,768]{1,0:T(8,128)}), f32[176,768]{1,0:T(8,128)}) %reduce-scatter.6.cloned.1.call-update) | async-done | bytes 540688 | tf_op jit(solution)/shard_map/while/body/eval_jaxpr/reduce_scatter | solution.py:124
  437.7 28.0 %all-gather.9.cloned.1.call-done = bf16[704,768]{1,0:T(8,128)(2,1)} async-done(((bf16[176,768]{1,0:T(8,128)(2,1)}), bf16[704,768]{1,0:T(8,128)(2,1)}) %all-gather.9.cloned.1.call-update) | async-done | bytes 1081360 | tf_op jit(solution)/shard_map/while/body/eval_jaxpr/all_gather | solution.py:131
  472.2 44.6 %reduce-scatter.8.cloned.1.call-done = f32[176,768]{1,0:T(8,128)} async-done(((f32[704,768]{1,0:T(8,128)}), f32[176,768]{1,0:T(8,128)}) %reduce-scatter.8.cloned.1.call-update) | async-done | bytes 540688 | tf_op jit(solution)/shard_map/while/body/eval_jaxpr/reduce_scatter | solution.py:147
  536.4 28.9 %all-gather.7.cloned.1.call-done = bf16[704,768]{1,0:T(8,128)(2,1)} async-done(((bf16[176,768]{1,0:T(8,128)(2,1)}), bf16[704,768]{1,0:T(8,128)(2,1)}) %all-gather.7.cloned.1.call-update) | async-done | bytes 1081360 | tf_op jit(solution)/shard_map/while/body/eval_jaxpr/all_gather | solution.py:122
  603.4 13.8 fusion.255
  625.1 43.8 %reduce-scatter.6.cloned.1.call-done = f32[176,768]{1,0:T(8,128)} async-done(((f32[704,768]{1,0:T(8,128)}), f32[176,768]{1,0:T(8,128)}) %reduce-scatter.6.cloned.1.call-update) | async-done | bytes 540688 | tf_op jit(solution)/shard_map/while/body/eval_jaxpr/reduce_scatter | solution.py:124
  671.3 28.0 %all-gather.9.cloned.1.call-done = bf16[704,768]{1,0:T(8,128)(2,1)} async-done(((bf16[176,768]{1,0:T(8,128)(2,1)}), bf16[704,768]{1,0:T(8,128)(2,1)}) %all-gather.9.cloned.1.call-update) | async-done | bytes 1081360 | tf_op jit(solution)/shard_map/while/body/eval_jaxpr/all_gather | solution.py:131
  705.8 44.6 %reduce-scatter.8.cloned.1.call-done = f32[176,768]{1,0:T(8,128)} async-done(((f32[704,768]{1,0:T(8,128)}), f32[176,768]{1,0:T(8,128)}) %reduce-scatter.8.cloned.1.call-update) | async-done | bytes 540688 | tf_op jit(solution)/shard_map/while/body/eval_jaxpr/reduce_scatter | solution.py:147
  753.6 1268.6 %while.52 = (s32[]{:T(128)}, f32[176,768]{1,0:T(8,128)}, f32[2,176,768]{2,1,0:T(8,128)}, f32[768]{0:T(1024)}, f32[768]{0:T(1024)}, /*index=5*/f32[768,576]{0,1:T...) while((s32[]{:T(128)}, f32[176,768]{1,0:T(8,128)}, ...), condition=%wide.region_39.40_spmd.clone, body=%wide.region_9.39_spmd.clone.sunk | while | flops 50368700416 | bytes 605911616 | solution.py:343
  759.0 25.9 %all-gather.11.cloned.1.call-done = bf16[704,768]{1,0:T(8,128)(2,1)} async-done(((bf16[176,768]{1,0:T(8,128)(2,1)}), bf16[704,768]{1,0:T(8,128)(2,1)}) %all-gather.11.cloned.1.call-update) | async-done | bytes 1081360 | tf_op jit(solution)/shard_map/while/body/eval_jaxpr/all_gather | solution.py:122
  826.6 13.9 fusion.299
  850.3 43.2 %reduce-scatter.10.cloned.1.call-done = f32[176,768]{1,0:T(8,128)} async-done(((f32[704,768]{1,0:T(8,128)}), f32[176,768]{1,0:T(8,128)}) %reduce-scatter.10.cloned.1.call-update) | async-done | bytes 540688 | tf_op jit(solution)/shard_map/while/body/eval_jaxpr/reduce_scatter | solution.py:124
  898.6 14.5 collective-permute-done.1
  931.1 23.5 %all-gather.15.cloned.1.call-done = bf16[704,768]{1,0:T(8,128)(2,1)} async-done(((bf16[176,768]{1,0:T(8,128)(2,1)}), bf16[704,768]{1,0:T(8,128)(2,1)}) %all-gather.15.cloned.1.call-update) | async-done | bytes 1081360 | tf_op jit(solution)/shard_map/while/body/eval_jaxpr/all_gather | solution.py:174
  964.5 44.5 %reduce-scatter.12.cloned.1.call-done = f32[176,768]{1,0:T(8,128)} async-done(((f32[704,768]{1,0:T(8,128)}), f32[176,768]{1,0:T(8,128)}) %reduce-scatter.12.cloned.1.call-update) | async-done | bytes 540688 | tf_op jit(solution)/shard_map/while/body/eval_jaxpr/reduce_scatter | solution.py:182
  1023.1 20.0 all-gather.17.cloned.1.call-done
  1085.0 14.8 convolution_bitcast_fusion.20
  1144.2 26.5 %reduce-scatter.14.cloned.1.call-done = f32[176,768]{1,0:T(8,128)} async-done(((f32[704,768]{1,0:T(8,128)}), f32[176,768]{1,0:T(8,128)}) %reduce-scatter.14.cloned.1.call-update) | async-done | bytes 540688 | tf_op jit(solution)/shard_map/while/body/eval_jaxpr/reduce_scatter | solution.py:199
  1181.1 25.9 %all-gather.11.cloned.1.call-done = bf16[704,768]{1,0:T(8,128)(2,1)} async-done(((bf16[176,768]{1,0:T(8,128)(2,1)}), bf16[704,768]{1,0:T(8,128)(2,1)}) %all-gather.11.cloned.1.call-update) | async-done | bytes 1081360 | tf_op jit(solution)/shard_map/while/body/eval_jaxpr/all_gather | solution.py:122
  1248.6 13.9 fusion.299
  1272.3 43.3 %reduce-scatter.10.cloned.1.call-done = f32[176,768]{1,0:T(8,128)} async-done(((f32[704,768]{1,0:T(8,128)}), f32[176,768]{1,0:T(8,128)}) %reduce-scatter.10.cloned.1.call-update) | async-done | bytes 540688 | tf_op jit(solution)/shard_map/while/body/eval_jaxpr/reduce_scatter | solution.py:124
  1321.7 14.4 collective-permute-done.1
  1353.2 23.7 %all-gather.15.cloned.1.call-done = bf16[704,768]{1,0:T(8,128)(2,1)} async-done(((bf16[176,768]{1,0:T(8,128)(2,1)}), bf16[704,768]{1,0:T(8,128)(2,1)}) %all-gather.15.cloned.1.call-update) | async-done | bytes 1081360 | tf_op jit(solution)/shard_map/while/body/eval_jaxpr/all_gather | solution.py:174
  1386.7 44.5 %reduce-scatter.12.cloned.1.call-done = f32[176,768]{1,0:T(8,128)} async-done(((f32[704,768]{1,0:T(8,128)}), f32[176,768]{1,0:T(8,128)}) %reduce-scatter.12.cloned.1.call-update) | async-done | bytes 540688 | tf_op jit(solution)/shard_map/while/body/eval_jaxpr/reduce_scatter | solution.py:182
  1445.3 20.0 all-gather.17.cloned.1.call-done
  1507.2 14.8 convolution_bitcast_fusion.20
  1569.3 23.5 %reduce-scatter.14.cloned.1.call-done = f32[176,768]{1,0:T(8,128)} async-done(((f32[704,768]{1,0:T(8,128)}), f32[176,768]{1,0:T(8,128)}) %reduce-scatter.14.cloned.1.call-update) | async-done | bytes 540688 | tf_op jit(solution)/shard_map/while/body/eval_jaxpr/reduce_scatter | solution.py:199
  1603.3 25.9 %all-gather.11.cloned.1.call-done = bf16[704,768]{1,0:T(8,128)(2,1)} async-done(((bf16[176,768]{1,0:T(8,128)(2,1)}), bf16[704,768]{1,0:T(8,128)(2,1)}) %all-gather.11.cloned.1.call-update) | async-done | bytes 1081360 | tf_op jit(solution)/shard_map/while/body/eval_jaxpr/all_gather | solution.py:122
  1670.8 13.9 fusion.299
  1694.5 43.2 %reduce-scatter.10.cloned.1.call-done = f32[176,768]{1,0:T(8,128)} async-done(((f32[704,768]{1,0:T(8,128)}), f32[176,768]{1,0:T(8,128)}) %reduce-scatter.10.cloned.1.call-update) | async-done | bytes 540688 | tf_op jit(solution)/shard_map/while/body/eval_jaxpr/reduce_scatter | solution.py:124
  1743.9 14.5 collective-permute-done.1
  1775.4 23.5 %all-gather.15.cloned.1.call-done = bf16[704,768]{1,0:T(8,128)(2,1)} async-done(((bf16[176,768]{1,0:T(8,128)(2,1)}), bf16[704,768]{1,0:T(8,128)(2,1)}) %all-gather.15.cloned.1.call-update) | async-done | bytes 1081360 | tf_op jit(solution)/shard_map/while/body/eval_jaxpr/all_gather | solution.py:174
  1808.7 44.5 %reduce-scatter.12.cloned.1.call-done = f32[176,768]{1,0:T(8,128)} async-done(((f32[704,768]{1,0:T(8,128)}), f32[176,768]{1,0:T(8,128)}) %reduce-scatter.12.cloned.1.call-update) | async-done | bytes 540688 | tf_op jit(solution)/shard_map/while/body/eval_jaxpr/reduce_scatter | solution.py:182
  1867.3 20.0 all-gather.17.cloned.1.call-done
  1929.2 14.8 convolution_bitcast_fusion.20
  1991.4 23.5 %reduce-scatter.14.cloned.1.call-done = f32[176,768]{1,0:T(8,128)} async-done(((f32[704,768]{1,0:T(8,128)}), f32[176,768]{1,0:T(8,128)}) %reduce-scatter.14.cloned.1.call-update) | async-done | bytes 540688 | tf_op jit(solution)/shard_map/while/body/eval_jaxpr/reduce_scatter | solution.py:199
  2029.7 33.8 %all-reduce.34 = (f32[1,768]{1,0:T(1,128)}, f32[1,768]{1,0:T(1,128)}) all-reduce(f32[1,768]{1,0:T(1,128)S(1)} %broadcast_in_dim.232, f32[1,768]{1,0:T(1,128)S(1)} %broadcast_in_dim.237), channel_id=1, replica_groups=mesh['section'=2,'dp'=4,'tensor'=4] {'dp','tensor'}, use_global_device_ids=true, to_apply=%region_40.41 | all-reduce | flops 1536 | bytes 12288 | tf_op jit(solution)/shard_map/psum | solution.py:351
  2075.9 143.5 %all-reduce.39.cloned.1.call-done = (f32[1,768,3,192]{1,3,2,0:T(8,128)}, f32[1,2,705,192]{2,3,1,0:T(8,128)}, f32[1,192,768]{2,1,0:T(8,128)}, f32[1,768,2,768]{3,2,1,0:T(2,128)}, f32[1,768,768]{2,1,0:T(8,128)}) async-done(((f32[1,768,3,192]{1,3,2,0:T(8,128)}, f32[1,2,705,192]{2,3,1,0:T(8,128)}, f32[1,192,768]{2,1,0:T(8,128)}, f32[1,768,2,768]{3,2,1,0:T(2,128)}, f32[1,768,768]{2,1,0:T(8,128)}), ...) | async-done | bytes 10520080 | tf_op jit(solution)/shard_map/psum | solution.py:347
  (1307 shorter events, 848.8 us)
Async XLA Ops:
  48.4 49.6 %all-gather.7.cloned.1.call-start = ((), (), s32[]{:S(2)}) async-start(), calls=%async_computation.6 | async-start | bytes 1351680 | tf_op jit(solution)/shard_map/while/body/eval_jaxpr/all_gather | solution.py:122
  48.5 16.4 collective-permute-start
  67.2 134.5 %reduce-scatter.6.cloned.1.call-start = ((), (), s32[]{:S(2)}) async-start(), calls=%async_computation.7 | async-start | bytes 2703360 | tf_op jit(solution)/shard_map/while/body/eval_jaxpr/reduce_scatter | solution.py:124
  157.1 74.9 %all-gather.9.cloned.1.call-start = ((), (), s32[]{:S(2)}) async-start(), calls=%async_computation.8 | async-start | bytes 1351680 | tf_op jit(solution)/shard_map/while/body/eval_jaxpr/all_gather | solution.py:131
  204.0 79.2 %reduce-scatter.8.cloned.1.call-start = ((), (), s32[]{:S(2)}) async-start(), calls=%async_computation.9 | async-start | bytes 2703360 | tf_op jit(solution)/shard_map/while/body/eval_jaxpr/reduce_scatter | solution.py:147
  238.6 44.6 %copy-start.42 = (f32[2,176,768]{2,1,0:T(8,128)S(1)}, f32[2,176,768]{2,1,0:T(8,128)}, u32[]{:S(2)}) copy-start(f32[2,176,768]{2,1,0:T(8,128)} %get-tuple-element.1576) | copy-start | bytes 3244036 | tf_op jit(solution)/shard_map/while
  285.4 46.3 %all-gather.7.cloned.1.call-start = ((), (), s32[]{:S(2)}) async-start(), calls=%async_computation.6 | async-start | bytes 1351680 | tf_op jit(solution)/shard_map/while/body/eval_jaxpr/all_gather | solution.py:122
  285.4 14.7 collective-permute-start
  302.5 132.9 %reduce-scatter.6.cloned.1.call-start = ((), (), s32[]{:S(2)}) async-start(), calls=%async_computation.7 | async-start | bytes 2703360 | tf_op jit(solution)/shard_map/while/body/eval_jaxpr/reduce_scatter | solution.py:124
  390.7 74.9 %all-gather.9.cloned.1.call-start = ((), (), s32[]{:S(2)}) async-start(), calls=%async_computation.8 | async-start | bytes 1351680 | tf_op jit(solution)/shard_map/while/body/eval_jaxpr/all_gather | solution.py:131
  437.6 79.2 %reduce-scatter.8.cloned.1.call-start = ((), (), s32[]{:S(2)}) async-start(), calls=%async_computation.9 | async-start | bytes 2703360 | tf_op jit(solution)/shard_map/while/body/eval_jaxpr/reduce_scatter | solution.py:147
  472.2 44.6 %copy-start.42 = (f32[2,176,768]{2,1,0:T(8,128)S(1)}, f32[2,176,768]{2,1,0:T(8,128)}, u32[]{:S(2)}) copy-start(f32[2,176,768]{2,1,0:T(8,128)} %get-tuple-element.1576) | copy-start | bytes 3244036 | tf_op jit(solution)/shard_map/while
  519.0 46.3 %all-gather.7.cloned.1.call-start = ((), (), s32[]{:S(2)}) async-start(), calls=%async_computation.6 | async-start | bytes 1351680 | tf_op jit(solution)/shard_map/while/body/eval_jaxpr/all_gather | solution.py:122
  519.0 14.7 collective-permute-start
  536.1 132.9 %reduce-scatter.6.cloned.1.call-start = ((), (), s32[]{:S(2)}) async-start(), calls=%async_computation.7 | async-start | bytes 2703360 | tf_op jit(solution)/shard_map/while/body/eval_jaxpr/reduce_scatter | solution.py:124
  624.3 74.9 %all-gather.9.cloned.1.call-start = ((), (), s32[]{:S(2)}) async-start(), calls=%async_computation.8 | async-start | bytes 1351680 | tf_op jit(solution)/shard_map/while/body/eval_jaxpr/all_gather | solution.py:131
  671.2 79.2 %reduce-scatter.8.cloned.1.call-start = ((), (), s32[]{:S(2)}) async-start(), calls=%async_computation.9 | async-start | bytes 2703360 | tf_op jit(solution)/shard_map/while/body/eval_jaxpr/reduce_scatter | solution.py:147
  705.8 44.6 %copy-start.42 = (f32[2,176,768]{2,1,0:T(8,128)S(1)}, f32[2,176,768]{2,1,0:T(8,128)}, u32[]{:S(2)}) copy-start(f32[2,176,768]{2,1,0:T(8,128)} %get-tuple-element.1576) | copy-start | bytes 3244036 | tf_op jit(solution)/shard_map/while
  754.1 33.3 %copy-start.5 = (f32[2,176,768]{2,1,0:T(8,128)}, f32[2,176,768]{2,1,0:T(8,128)S(1)}, u32[]{:S(2)}) copy-start(f32[2,176,768]{2,1,0:T(8,128)S(1)} %get-tuple-element.1720) | copy-start | bytes 3244036 | tf_op jit(solution)/shard_map/while
  754.1 33.3 %copy-start.59 = (s32[2,704]{1,0:T(2,128)}, s32[2,704]{1,0:T(2,128)S(1)}, u32[]{:S(2)}) copy-start(s32[2,704]{1,0:T(2,128)S(1)} %get-tuple-element.1724) | copy-start | bytes 16900 | tf_op jit(solution)/shard_map/while
  754.1 33.3 %copy-start.86 = (f32[1,768]{1,0:T(1,128)}, f32[1,768]{1,0:T(1,128)S(1)}, u32[]{:S(2)}) copy-start(f32[1,768]{1,0:T(1,128)S(1)} %get-tuple-element.1722) | copy-start | bytes 9220 | tf_op jit(solution)/shard_map/while
  754.1 33.3 %copy-start.88 = (f32[3,192]{1,0:T(4,128)}, f32[3,192]{1,0:T(4,128)S(1)}, u32[]{:S(2)}) copy-start(f32[3,192]{1,0:T(4,128)S(1)} %get-tuple-element.1728) | copy-start | bytes 6916 | tf_op jit(solution)/shard_map/while
  754.2 30.8 %all-gather.11.cloned.1.call-start = ((), (), s32[]{:S(2)}) async-start(), calls=%async_computation.10 | async-start | bytes 1351680 | tf_op jit(solution)/shard_map/while/body/eval_jaxpr/all_gather | solution.py:122
  756.9 136.6 %reduce-scatter.10.cloned.1.call-start = ((), (), s32[]{:S(2)}) async-start(), calls=%async_computation.11 | async-start | bytes 2703360 | tf_op jit(solution)/shard_map/while/body/eval_jaxpr/reduce_scatter | solution.py:124
  849.0 76.2 %all-gather.13.cloned.1.call-start = ((), (), s32[]{:S(2)}) async-start(), calls=%async_computation.12 | async-start | bytes 1351680 | tf_op jit(solution)/shard_map/while/body/eval_jaxpr/all_gather | solution.py:131
  897.2 57.4 %all-gather.15.cloned.1.call-start = ((), (), s32[]{:S(2)}) async-start(), calls=%async_computation.13 | async-start | bytes 1351680 | tf_op jit(solution)/shard_map/while/body/eval_jaxpr/all_gather | solution.py:174
  897.3 15.8 collective-permute-start.1
  915.6 93.4 %reduce-scatter.12.cloned.1.call-start = ((), (), s32[]{:S(2)}) async-start(), calls=%async_computation.14 | async-start | bytes 2703360 | tf_op jit(solution)/shard_map/while/body/eval_jaxpr/reduce_scatter | solution.py:182
  964.5 78.6 %all-gather.17.cloned.1.call-start = ((), (), s32[]{:S(2)}) async-start(), calls=%async_computation.15 | async-start | bytes 1351680 | tf_op jit(solution)/shard_map/while/body/eval_jaxpr/all_gather | solution.py:190
  1015.1 155.6 %reduce-scatter.14.cloned.1.call-start = ((), (), s32[]{:S(2)}) async-start(), calls=%async_computation.16 | async-start | bytes 2703360 | tf_op jit(solution)/shard_map/while/body/eval_jaxpr/reduce_scatter | solution.py:199
  1176.2 30.7 %all-gather.11.cloned.1.call-start = ((), (), s32[]{:S(2)}) async-start(), calls=%async_computation.10 | async-start | bytes 1351680 | tf_op jit(solution)/shard_map/while/body/eval_jaxpr/all_gather | solution.py:122
  1179.0 136.6 %reduce-scatter.10.cloned.1.call-start = ((), (), s32[]{:S(2)}) async-start(), calls=%async_computation.11 | async-start | bytes 2703360 | tf_op jit(solution)/shard_map/while/body/eval_jaxpr/reduce_scatter | solution.py:124
  1271.0 76.3 %all-gather.13.cloned.1.call-start = ((), (), s32[]{:S(2)}) async-start(), calls=%async_computation.12 | async-start | bytes 1351680 | tf_op jit(solution)/shard_map/while/body/eval_jaxpr/all_gather | solution.py:131
  1319.3 57.6 %all-gather.15.cloned.1.call-start = ((), (), s32[]{:S(2)}) async-start(), calls=%async_computation.13 | async-start | bytes 1351680 | tf_op jit(solution)/shard_map/while/body/eval_jaxpr/all_gather | solution.py:174
  1320.4 15.8 collective-permute-start.1
  1338.7 92.5 %reduce-scatter.12.cloned.1.call-start = ((), (), s32[]{:S(2)}) async-start(), calls=%async_computation.14 | async-start | bytes 2703360 | tf_op jit(solution)/shard_map/while/body/eval_jaxpr/reduce_scatter | solution.py:182
  1386.6 78.6 %all-gather.17.cloned.1.call-start = ((), (), s32[]{:S(2)}) async-start(), calls=%async_computation.15 | async-start | bytes 1351680 | tf_op jit(solution)/shard_map/while/body/eval_jaxpr/all_gather | solution.py:190
  1437.3 155.6 %reduce-scatter.14.cloned.1.call-start = ((), (), s32[]{:S(2)}) async-start(), calls=%async_computation.16 | async-start | bytes 2703360 | tf_op jit(solution)/shard_map/while/body/eval_jaxpr/reduce_scatter | solution.py:199
  1598.4 30.8 %all-gather.11.cloned.1.call-start = ((), (), s32[]{:S(2)}) async-start(), calls=%async_computation.10 | async-start | bytes 1351680 | tf_op jit(solution)/shard_map/while/body/eval_jaxpr/all_gather | solution.py:122
  1601.2 136.6 %reduce-scatter.10.cloned.1.call-start = ((), (), s32[]{:S(2)}) async-start(), calls=%async_computation.11 | async-start | bytes 2703360 | tf_op jit(solution)/shard_map/while/body/eval_jaxpr/reduce_scatter | solution.py:124
  1693.2 76.2 %all-gather.13.cloned.1.call-start = ((), (), s32[]{:S(2)}) async-start(), calls=%async_computation.12 | async-start | bytes 1351680 | tf_op jit(solution)/shard_map/while/body/eval_jaxpr/all_gather | solution.py:131
  1741.4 57.4 %all-gather.15.cloned.1.call-start = ((), (), s32[]{:S(2)}) async-start(), calls=%async_computation.13 | async-start | bytes 1351680 | tf_op jit(solution)/shard_map/while/body/eval_jaxpr/all_gather | solution.py:174
  1742.6 15.8 collective-permute-start.1
  1760.9 92.4 %reduce-scatter.12.cloned.1.call-start = ((), (), s32[]{:S(2)}) async-start(), calls=%async_computation.14 | async-start | bytes 2703360 | tf_op jit(solution)/shard_map/while/body/eval_jaxpr/reduce_scatter | solution.py:182
  1808.7 78.6 %all-gather.17.cloned.1.call-start = ((), (), s32[]{:S(2)}) async-start(), calls=%async_computation.15 | async-start | bytes 1351680 | tf_op jit(solution)/shard_map/while/body/eval_jaxpr/all_gather | solution.py:190
  1859.3 155.6 %reduce-scatter.14.cloned.1.call-start = ((), (), s32[]{:S(2)}) async-start(), calls=%async_computation.16 | async-start | bytes 2703360 | tf_op jit(solution)/shard_map/while/body/eval_jaxpr/reduce_scatter | solution.py:199
  2022.2 197.2 %all-reduce.39.cloned.1.call-start = ((), (), s32[]{:S(2)}) async-start(), calls=%async_computation.5 | async-start | bytes 21233664 | tf_op jit(solution)/shard_map/psum | solution.py:347
  2028.9 34.6 %copy-start.124 = (f32[2,192]{1,0:T(2,128)S(1)}, f32[2,192]{1,0:T(2,128)}, u32[]{:S(2)}) copy-start(f32[2,192]{1,0:T(2,128)} %get-tuple-element.559) | copy-start | bytes 4612
  (386 other events, 2580.7 us)
Sparse Core Ops, SparseCore 0:
  67.3 30.7 all-gather.6
  157.2 44.4 reduce-scatter.5
  204.1 27.8 all-gather.8
  238.7 44.4 reduce-scatter.7
  302.6 29.0 all-gather.6
  390.9 44.4 reduce-scatter.5
  437.7 27.8 all-gather.8
  472.3 44.4 reduce-scatter.7
  536.2 29.0 all-gather.6
  624.5 44.4 reduce-scatter.5
  671.3 27.8 all-gather.8
  706.0 44.4 reduce-scatter.7
  757.0 27.8 all-gather.10
  849.1 44.4 reduce-scatter.9
  897.3 27.8 all-gather.12
  926.6 27.9 all-gather.14
  964.6 44.4 reduce-scatter.11
  1015.2 27.8 all-gather.16
  1126.2 44.4 reduce-scatter.13
  1179.1 27.8 all-gather.10
  1271.1 44.4 reduce-scatter.9
  1319.4 27.8 all-gather.12
  1348.8 27.9 all-gather.14
  1386.8 44.4 reduce-scatter.11
  1437.4 27.8 all-gather.16
  1548.4 44.4 reduce-scatter.13
  1601.3 27.8 all-gather.10
  1693.3 44.4 reduce-scatter.9
  1741.6 27.8 all-gather.12
  1770.9 27.9 all-gather.14
  1808.8 44.4 reduce-scatter.11
  1859.4 27.8 all-gather.16
  1970.4 44.4 reduce-scatter.13
Sparse Core Ops, SparseCore 1:
  2029.0 190.3 all-reduce.38
where the time goes:
time: 2250 us; the launch traced here: 2240 us
  waiting for transfers between devices  1230 us (55%)
  matrix products  430 us (19%)
  local copies, waits for them, and re-layouts  279 us (12%)
  other arithmetic  208 us (9%)
  blocking collectives  46.2 us (2%)
    reduce_scatter x6, waiting for transfers between devices, run_layer(): lax.psum_scatter(jnp.dot(mixed_low, w_out, preferred_element_type=jnp.flo...  261 us
    all_gather x6, waiting for transfers between devices, run_layer(): lax.all_gather(normed.astype(jnp.bfloat16), 'tensor', axis=0, tiled=True)  166 us
    psum x1, waiting for transfers between devices, per_device(): lax.psum((sum_in, sum_short, sum_cond, sum_spec, sum_gain, sum_out, sum_g...  143 us
    reduce_scatter x3, waiting for transfers between devices, run_layer(): lax.psum_scatter(jnp.dot(act_low, w_down, preferred_element_type=jnp.floa...  134 us
    reduce_scatter x3, waiting for transfers between devices, back_layer(): lax.psum_scatter(jnp.einsum('lf,df->ld', piece, w_gate_up, preferred_elem...  134 us
    dot_general x9, matrix products, orchid_mix(): jnp.dot(inverse_table, joined, precision=highest)  124 us
    dot_general x9, matrix products, orchid_mix(): jnp.dot(forward_table, pieces, precision=highest)  123 us
    all_gather x6, waiting for transfers between devices, run_layer(): lax.all_gather(normed_two.astype(jnp.bfloat16), 'tensor', axis=0, tiled=T...  110 us
  transfers between devices with their start and end apart: 40, of which 40 were waited for; matrix products, arithmetic and copies ran while one was open for 5% of the time, Pallas kernels for 0%

commit v1 on v0

--- a/solution.py
+++ b/solution.py
@@ -4,9 +4,17 @@
 import jax.numpy as jnp
 from jax import lax
 from jax.sharding import PartitionSpec as P
+from jax.lax import all_to_all, axis_size
 
 SEGS = 4
 highest = lax.Precision.HIGHEST
+
+
+def assign_ratios_in(frame, named_axis):
+    current_arr = jnp.concatenate(
+        all_to_all(jnp.stack([frame] * axis_size(named_axis)), named_axis, 0, 0), axis=0
+    )
+    return current_arr
 
 
 def from_behind(shard, axis, by):
@@ -187,7 +195,7 @@
     )
     grad_hidden_part, grad_gain_two = norm_pull_two(grad_normed_two)
     grad_hidden = grad_out + grad_hidden_part
-    grad_mix_rows = lax.all_gather(grad_hidden.astype(jnp.bfloat16), "tensor", axis=0, tiled=True)
+    grad_mix_rows = assign_ratios_in(grad_hidden.astype(jnp.bfloat16), "tensor")
     grad_mixed = jnp.einsum("ld,cd->lc", grad_mix_rows, w_out, preferred_element_type=jnp.float32)
     grad_w_out = jnp.einsum(
         "lc,ld->cd", mixed_low, grad_mix_rows, preferred_element_type=jnp.float32

time: 2250 us -> 2250 us (level)
    all_gather x3 -> x0, waiting for transfers between devices: 59.9 us -> none  [back_layer(): lax.all_gather(grad_hidden.astype(jnp.bfloat16), 'tensor', axis=0, tiled=...]
    all_to_all x0 -> x3, waiting for transfers between devices: none -> 55.6 us  [assign_ratios_in(): all_to_all(jnp.stack([frame] * axis_size(named_axis)), named_axis, 0, 0)]
    while x750 -> x744, local copies, waits for them, and re-layouts: 61.9 us -> 59.3 us
where the time goes in v1:
time: 2250 us
  waiting for transfers between devices  1220 us (54%)
  matrix products  436 us (19%)
  local copies, waits for them, and re-layouts  280 us (12%)
  other arithmetic  206 us (9%)
  blocking collectives  46.2 us (2%)
  starting transfers between devices  29.6 us (1%)
    reduce_scatter x6, waiting for transfers between devices, run_layer(): lax.psum_scatter(jnp.dot(mixed_low, w_out, preferred_element_type=jnp.flo...  261 us
    all_gather x6, waiting for transfers between devices, run_layer(): lax.all_gather(normed.astype(jnp.bfloat16), 'tensor', axis=0, tiled=True)  166 us
    psum x1, waiting for transfers between devices, per_device(): lax.psum((sum_in, sum_short, sum_cond, sum_spec, sum_gain, sum_out, sum_g...  143 us
    reduce_scatter x3, waiting for transfers between devices, back_layer(): lax.psum_scatter(jnp.einsum('lf,df->ld', piece, w_gate_up, preferred_elem...  134 us
    reduce_scatter x3, waiting for transfers between devices, run_layer(): lax.psum_scatter(jnp.dot(act_low, w_down, preferred_element_type=jnp.floa...  134 us
    dot_general x9, matrix products, orchid_mix(): jnp.dot(inverse_table, joined, precision=highest)  124 us
    dot_general x9, matrix products, orchid_mix(): jnp.dot(forward_table, pieces, precision=highest)  123 us
    all_gather x6, waiting for transfers between devices, run_layer(): lax.all_gather(normed_two.astype(jnp.bfloat16), 'tensor', axis=0, tiled=T...  110 us
  transfers between devices with their start and end apart: 40, of which 40 were waited for; matrix products, arithmetic and copies ran while one was open for 5% of the time, Pallas kernels for 0%

profile of v1, /device:TPU:0, one launch (start us, length us, event | category | flops | bytes accessed | tf_op | source)
XLA Modules:
  0.0 2245.5 jit_solution(2205921302178640751)
XLA Ops:
  48.2 704.5 %while.51 = (s32[]{:T(128)}, f32[176,768]{1,0:T(8,128)S(1)}, f32[2,176,768]{2,1,0:T(8,128)S(1)}, f32[2,176,768]{2,1,0:T(8,128)}, pred[]{:T(512)}, /*index=5*/s32...) while((s32[]{:T(128)}, f32[176,768]{1,0:T(8,128)S(1)}, ...), condition=%wide.region_8.9_spmd.clone, body=%wide.region_0.8_spmd.clone.sunk | while | flops 23922319360 | bytes 190306960 | solution.py:291
  67.5 30.6 %all-gather.6.cloned.1.call-done = bf16[704,768]{1,0:T(8,128)(2,1)} async-done(((bf16[176,768]{1,0:T(8,128)(2,1)}), bf16[704,768]{1,0:T(8,128)(2,1)}) %all-gather.6.cloned.1.call-update) | async-done | bytes 1081360 | tf_op jit(solution)/shard_map/while/body/eval_jaxpr/all_gather | solution.py:130
  113.5 13.8 convolution_bitcast_fusion.15
  136.2 13.9 fusion.255
  157.9 43.8 %reduce-scatter.6.cloned.1.call-done = f32[176,768]{1,0:T(8,128)} async-done(((f32[704,768]{1,0:T(8,128)}), f32[176,768]{1,0:T(8,128)}) %reduce-scatter.6.cloned.1.call-update) | async-done | bytes 540688 | tf_op jit(solution)/shard_map/while/body/eval_jaxpr/reduce_scatter | solution.py:132
  204.1 27.9 %all-gather.8.cloned.1.call-done = bf16[704,768]{1,0:T(8,128)(2,1)} async-done(((bf16[176,768]{1,0:T(8,128)(2,1)}), bf16[704,768]{1,0:T(8,128)(2,1)}) %all-gather.8.cloned.1.call-update) | async-done | bytes 1081360 | tf_op jit(solution)/shard_map/while/body/eval_jaxpr/all_gather | solution.py:139
  238.7 44.6 %reduce-scatter.8.cloned.1.call-done = f32[176,768]{1,0:T(8,128)} async-done(((f32[704,768]{1,0:T(8,128)}), f32[176,768]{1,0:T(8,128)}) %reduce-scatter.8.cloned.1.call-update) | async-done | bytes 540688 | tf_op jit(solution)/shard_map/while/body/eval_jaxpr/reduce_scatter | solution.py:155
  302.8 28.9 %all-gather.6.cloned.1.call-done = bf16[704,768]{1,0:T(8,128)(2,1)} async-done(((bf16[176,768]{1,0:T(8,128)(2,1)}), bf16[704,768]{1,0:T(8,128)(2,1)}) %all-gather.6.cloned.1.call-update) | async-done | bytes 1081360 | tf_op jit(solution)/shard_map/while/body/eval_jaxpr/all_gather | solution.py:130
  347.2 13.8 convolution_bitcast_fusion.15
  369.9 13.9 fusion.255
  391.6 43.8 %reduce-scatter.6.cloned.1.call-done = f32[176,768]{1,0:T(8,128)} async-done(((f32[704,768]{1,0:T(8,128)}), f32[176,768]{1,0:T(8,128)}) %reduce-scatter.6.cloned.1.call-update) | async-done | bytes 540688 | tf_op jit(solution)/shard_map/while/body/eval_jaxpr/reduce_scatter | solution.py:132
  437.8 27.9 %all-gather.8.cloned.1.call-done = bf16[704,768]{1,0:T(8,128)(2,1)} async-done(((bf16[176,768]{1,0:T(8,128)(2,1)}), bf16[704,768]{1,0:T(8,128)(2,1)}) %all-gather.8.cloned.1.call-update) | async-done | bytes 1081360 | tf_op jit(solution)/shard_map/while/body/eval_jaxpr/all_gather | solution.py:139
  472.3 44.6 %reduce-scatter.8.cloned.1.call-done = f32[176,768]{1,0:T(8,128)} async-done(((f32[704,768]{1,0:T(8,128)}), f32[176,768]{1,0:T(8,128)}) %reduce-scatter.8.cloned.1.call-update) | async-done | bytes 540688 | tf_op jit(solution)/shard_map/while/body/eval_jaxpr/reduce_scatter | solution.py:155
  536.5 28.9 %all-gather.6.cloned.1.call-done = bf16[704,768]{1,0:T(8,128)(2,1)} async-done(((bf16[176,768]{1,0:T(8,128)(2,1)}), bf16[704,768]{1,0:T(8,128)(2,1)}) %all-gather.6.cloned.1.call-update) | async-done | bytes 1081360 | tf_op jit(solution)/shard_map/while/body/eval_jaxpr/all_gather | solution.py:130
  603.5 13.9 fusion.255
  625.2 43.8 %reduce-scatter.6.cloned.1.call-done = f32[176,768]{1,0:T(8,128)} async-done(((f32[704,768]{1,0:T(8,128)}), f32[176,768]{1,0:T(8,128)}) %reduce-scatter.6.cloned.1.call-update) | async-done | bytes 540688 | tf_op jit(solution)/shard_map/while/body/eval_jaxpr/reduce_scatter | solution.py:132
  671.4 27.9 %all-gather.8.cloned.1.call-done = bf16[704,768]{1,0:T(8,128)(2,1)} async-done(((bf16[176,768]{1,0:T(8,128)(2,1)}), bf16[704,768]{1,0:T(8,128)(2,1)}) %all-gather.8.cloned.1.call-update) | async-done | bytes 1081360 | tf_op jit(solution)/shard_map/while/body/eval_jaxpr/all_gather | solution.py:139
  706.0 44.6 %reduce-scatter.8.cloned.1.call-done = f32[176,768]{1,0:T(8,128)} async-done(((f32[704,768]{1,0:T(8,128)}), f32[176,768]{1,0:T(8,128)}) %reduce-scatter.8.cloned.1.call-update) | async-done | bytes 540688 | tf_op jit(solution)/shard_map/while/body/eval_jaxpr/reduce_scatter | solution.py:155
  753.8 1277.0 %while.52 = (s32[]{:T(128)}, f32[176,768]{1,0:T(8,128)}, f32[2,176,768]{2,1,0:T(8,128)}, f32[768]{0:T(1024)}, f32[768]{0:T(1024)}, /*index=5*/f32[768,576]{0,1:T...) while((s32[]{:T(128)}, f32[176,768]{1,0:T(8,128)}, ...), condition=%wide.region_39.40_spmd.clone, body=%wide.region_9.39_spmd.clone.sunk | while | flops 50368700416 | bytes 602126912 | solution.py:351
  759.2 25.9 %all-gather.10.cloned.1.call-done = bf16[704,768]{1,0:T(8,128)(2,1)} async-done(((bf16[176,768]{1,0:T(8,128)(2,1)}), bf16[704,768]{1,0:T(8,128)(2,1)}) %all-gather.10.cloned.1.call-update) | async-done | bytes 1081360 | tf_op jit(solution)/shard_map/while/body/eval_jaxpr/all_gather | solution.py:130
  826.7 13.9 fusion.299
  850.5 43.3 %reduce-scatter.10.cloned.1.call-done = f32[176,768]{1,0:T(8,128)} async-done(((f32[704,768]{1,0:T(8,128)}), f32[176,768]{1,0:T(8,128)}) %reduce-scatter.10.cloned.1.call-update) | async-done | bytes 540688 | tf_op jit(solution)/shard_map/while/body/eval_jaxpr/reduce_scatter | solution.py:132
  898.8 14.4 collective-permute-done.1
  931.3 23.5 %all-gather.14.cloned.1.call-done = bf16[704,768]{1,0:T(8,128)(2,1)} async-done(((bf16[176,768]{1,0:T(8,128)(2,1)}), bf16[704,768]{1,0:T(8,128)(2,1)}) %all-gather.14.cloned.1.call-update) | async-done | bytes 1081360 | tf_op jit(solution)/shard_map/while/body/eval_jaxpr/all_gather | solution.py:182
  964.7 44.6 %reduce-scatter.12.cloned.1.call-done = f32[176,768]{1,0:T(8,128)} async-done(((f32[704,768]{1,0:T(8,128)}), f32[176,768]{1,0:T(8,128)}) %reduce-scatter.12.cloned.1.call-update) | async-done | bytes 540688 | tf_op jit(solution)/shard_map/while/body/eval_jaxpr/reduce_scatter | solution.py:190
  1028.0 18.5 all-to-all-done
  1088.4 14.8 convolution_bitcast_fusion.20
  1148.3 25.2 %reduce-scatter.14.cloned.1.call-done = f32[176,768]{1,0:T(8,128)} async-done(((f32[704,768]{1,0:T(8,128)}), f32[176,768]{1,0:T(8,128)}) %reduce-scatter.14.cloned.1.call-update) | async-done | bytes 540688 | tf_op jit(solution)/shard_map/while/body/eval_jaxpr/reduce_scatter | solution.py:207
  1184.0 25.9 %all-gather.10.cloned.1.call-done = bf16[704,768]{1,0:T(8,128)(2,1)} async-done(((bf16[176,768]{1,0:T(8,128)(2,1)}), bf16[704,768]{1,0:T(8,128)(2,1)}) %all-gather.10.cloned.1.call-update) | async-done | bytes 1081360 | tf_op jit(solution)/shard_map/while/body/eval_jaxpr/all_gather | solution.py:130
  1251.5 13.9 fusion.299
  1275.3 43.2 %reduce-scatter.10.cloned.1.call-done = f32[176,768]{1,0:T(8,128)} async-done(((f32[704,768]{1,0:T(8,128)}), f32[176,768]{1,0:T(8,128)}) %reduce-scatter.10.cloned.1.call-update) | async-done | bytes 540688 | tf_op jit(solution)/shard_map/while/body/eval_jaxpr/reduce_scatter | solution.py:132
  1324.6 14.5 collective-permute-done.1
  1356.1 23.6 %all-gather.14.cloned.1.call-done = bf16[704,768]{1,0:T(8,128)(2,1)} async-done(((bf16[176,768]{1,0:T(8,128)(2,1)}), bf16[704,768]{1,0:T(8,128)(2,1)}) %all-gather.14.cloned.1.call-update) | async-done | bytes 1081360 | tf_op jit(solution)/shard_map/while/body/eval_jaxpr/all_gather | solution.py:182
  1389.6 44.6 %reduce-scatter.12.cloned.1.call-done = f32[176,768]{1,0:T(8,128)} async-done(((f32[704,768]{1,0:T(8,128)}), f32[176,768]{1,0:T(8,128)}) %reduce-scatter.12.cloned.1.call-update) | async-done | bytes 540688 | tf_op jit(solution)/shard_map/while/body/eval_jaxpr/reduce_scatter | solution.py:190
  1452.9 18.6 all-to-all-done
  1513.3 14.8 convolution_bitcast_fusion.20
  1576.2 22.3 reduce-scatter.14.cloned.1.call-done
  1608.9 25.9 %all-gather.10.cloned.1.call-done = bf16[704,768]{1,0:T(8,128)(2,1)} async-done(((bf16[176,768]{1,0:T(8,128)(2,1)}), bf16[704,768]{1,0:T(8,128)(2,1)}) %all-gather.10.cloned.1.call-update) | async-done | bytes 1081360 | tf_op jit(solution)/shard_map/while/body/eval_jaxpr/all_gather | solution.py:130
  1676.5 13.9 fusion.299
  1700.2 43.2 %reduce-scatter.10.cloned.1.call-done = f32[176,768]{1,0:T(8,128)} async-done(((f32[704,768]{1,0:T(8,128)}), f32[176,768]{1,0:T(8,128)}) %reduce-scatter.10.cloned.1.call-update) | async-done | bytes 540688 | tf_op jit(solution)/shard_map/while/body/eval_jaxpr/reduce_scatter | solution.py:132
  1749.6 14.5 collective-permute-done.1
  1781.1 23.6 %all-gather.14.cloned.1.call-done = bf16[704,768]{1,0:T(8,128)(2,1)} async-done(((bf16[176,768]{1,0:T(8,128)(2,1)}), bf16[704,768]{1,0:T(8,128)(2,1)}) %all-gather.14.cloned.1.call-update) | async-done | bytes 1081360 | tf_op jit(solution)/shard_map/while/body/eval_jaxpr/all_gather | solution.py:182
  1814.6 44.6 %reduce-scatter.12.cloned.1.call-done = f32[176,768]{1,0:T(8,128)} async-done(((f32[704,768]{1,0:T(8,128)}), f32[176,768]{1,0:T(8,128)}) %reduce-scatter.12.cloned.1.call-update) | async-done | bytes 540688 | tf_op jit(solution)/shard_map/while/body/eval_jaxpr/reduce_scatter | solution.py:190
  1877.8 18.6 all-to-all-done
  1938.3 14.8 convolution_bitcast_fusion.20
  2001.1 22.3 reduce-scatter.14.cloned.1.call-done
  2038.3 33.8 %all-reduce.34 = (f32[1,768]{1,0:T(1,128)}, f32[1,768]{1,0:T(1,128)}) all-reduce(f32[1,768]{1,0:T(1,128)S(1)} %broadcast_in_dim.232, f32[1,768]{1,0:T(1,128)S(1)} %broadcast_in_dim.237), channel_id=1, replica_groups=mesh['section'=2,'dp'=4,'tensor'=4] {'dp','tensor'}, use_global_device_ids=true, to_apply=%region_40.41 | all-reduce | flops 1536 | bytes 12288 | tf_op jit(solution)/shard_map/psum | solution.py:359
  2084.6 143.4 %all-reduce.39.cloned.1.call-done = (f32[1,768,3,192]{1,3,2,0:T(8,128)}, f32[1,2,705,192]{2,3,1,0:T(8,128)}, f32[1,192,768]{2,1,0:T(8,128)}, f32[1,768,2,768]{3,2,1,0:T(2,128)}, f32[1,768,768]{2,1,0:T(8,128)}) async-done(((f32[1,768,3,192]{1,3,2,0:T(8,128)}, f32[1,2,705,192]{2,3,1,0:T(8,128)}, f32[1,192,768]{2,1,0:T(8,128)}, f32[1,768,2,768]{3,2,1,0:T(2,128)}, f32[1,768,768]{2,1,0:T(8,128)}), ...) | async-done | bytes 10520080 | tf_op jit(solution)/shard_map/psum | solution.py:355
  (1301 shorter events, 865.1 us)
Async XLA Ops:
  48.4 49.6 %all-gather.6.cloned.1.call-start = ((), (), s32[]{:S(2)}) async-start(), calls=%async_computation.7 | async-start | bytes 1351680 | tf_op jit(solution)/shard_map/while/body/eval_jaxpr/all_gather | solution.py:130
  48.5 16.4 collective-permute-start
  67.2 134.6 %reduce-scatter.6.cloned.1.call-start = ((), (), s32[]{:S(2)}) async-start(), calls=%async_computation.8 | async-start | bytes 2703360 | tf_op jit(solution)/shard_map/while/body/eval_jaxpr/reduce_scatter | solution.py:132
  157.2 74.9 %all-gather.8.cloned.1.call-start = ((), (), s32[]{:S(2)}) async-start(), calls=%async_computation.9 | async-start | bytes 1351680 | tf_op jit(solution)/shard_map/while/body/eval_jaxpr/all_gather | solution.py:139
  204.1 79.2 %reduce-scatter.8.cloned.1.call-start = ((), (), s32[]{:S(2)}) async-start(), calls=%async_computation.10 | async-start | bytes 2703360 | tf_op jit(solution)/shard_map/while/body/eval_jaxpr/reduce_scatter | solution.py:155
  238.6 44.6 %copy-start.41 = (f32[2,176,768]{2,1,0:T(8,128)S(1)}, f32[2,176,768]{2,1,0:T(8,128)}, u32[]{:S(2)}) copy-start(f32[2,176,768]{2,1,0:T(8,128)} %get-tuple-element.1576) | copy-start | bytes 3244036 | tf_op jit(solution)/shard_map/while
  285.4 46.3 %all-gather.6.cloned.1.call-start = ((), (), s32[]{:S(2)}) async-start(), calls=%async_computation.7 | async-start | bytes 1351680 | tf_op jit(solution)/shard_map/while/body/eval_jaxpr/all_gather | solution.py:130
  285.5 14.7 collective-permute-start
  302.5 132.9 %reduce-scatter.6.cloned.1.call-start = ((), (), s32[]{:S(2)}) async-start(), calls=%async_computation.8 | async-start | bytes 2703360 | tf_op jit(solution)/shard_map/while/body/eval_jaxpr/reduce_scatter | solution.py:132
  390.8 74.9 %all-gather.8.cloned.1.call-start = ((), (), s32[]{:S(2)}) async-start(), calls=%async_computation.9 | async-start | bytes 1351680 | tf_op jit(solution)/shard_map/while/body/eval_jaxpr/all_gather | solution.py:139
  437.7 79.2 %reduce-scatter.8.cloned.1.call-start = ((), (), s32[]{:S(2)}) async-start(), calls=%async_computation.10 | async-start | bytes 2703360 | tf_op jit(solution)/shard_map/while/body/eval_jaxpr/reduce_scatter | solution.py:155
  472.3 44.6 %copy-start.41 = (f32[2,176,768]{2,1,0:T(8,128)S(1)}, f32[2,176,768]{2,1,0:T(8,128)}, u32[]{:S(2)}) copy-start(f32[2,176,768]{2,1,0:T(8,128)} %get-tuple-element.1576) | copy-start | bytes 3244036 | tf_op jit(solution)/shard_map/while
  519.1 46.3 %all-gather.6.cloned.1.call-start = ((), (), s32[]{:S(2)}) async-start(), calls=%async_computation.7 | async-start | bytes 1351680 | tf_op jit(solution)/shard_map/while/body/eval_jaxpr/all_gather | solution.py:130
  519.1 14.7 collective-permute-start
  536.2 132.9 %reduce-scatter.6.cloned.1.call-start = ((), (), s32[]{:S(2)}) async-start(), calls=%async_computation.8 | async-start | bytes 2703360 | tf_op jit(solution)/shard_map/while/body/eval_jaxpr/reduce_scatter | solution.py:132
  624.5 74.9 %all-gather.8.cloned.1.call-start = ((), (), s32[]{:S(2)}) async-start(), calls=%async_computation.9 | async-start | bytes 1351680 | tf_op jit(solution)/shard_map/while/body/eval_jaxpr/all_gather | solution.py:139
  671.4 79.2 %reduce-scatter.8.cloned.1.call-start = ((), (), s32[]{:S(2)}) async-start(), calls=%async_computation.10 | async-start | bytes 2703360 | tf_op jit(solution)/shard_map/while/body/eval_jaxpr/reduce_scatter | solution.py:155
  706.0 44.6 %copy-start.41 = (f32[2,176,768]{2,1,0:T(8,128)S(1)}, f32[2,176,768]{2,1,0:T(8,128)}, u32[]{:S(2)}) copy-start(f32[2,176,768]{2,1,0:T(8,128)} %get-tuple-element.1576) | copy-start | bytes 3244036 | tf_op jit(solution)/shard_map/while
  754.3 33.3 %copy-start.5 = (f32[2,176,768]{2,1,0:T(8,128)}, f32[2,176,768]{2,1,0:T(8,128)S(1)}, u32[]{:S(2)}) copy-start(f32[2,176,768]{2,1,0:T(8,128)S(1)} %get-tuple-element.1720) | copy-start | bytes 3244036 | tf_op jit(solution)/shard_map/while
  754.3 33.3 %copy-start.58 = (s32[2,704]{1,0:T(2,128)}, s32[2,704]{1,0:T(2,128)S(1)}, u32[]{:S(2)}) copy-start(s32[2,704]{1,0:T(2,128)S(1)} %get-tuple-element.1724) | copy-start | bytes 16900 | tf_op jit(solution)/shard_map/while
  754.3 33.3 %copy-start.85 = (f32[1,768]{1,0:T(1,128)}, f32[1,768]{1,0:T(1,128)S(1)}, u32[]{:S(2)}) copy-start(f32[1,768]{1,0:T(1,128)S(1)} %get-tuple-element.1722) | copy-start | bytes 9220 | tf_op jit(solution)/shard_map/while
  754.3 30.8 %all-gather.10.cloned.1.call-start = ((), (), s32[]{:S(2)}) async-start(), calls=%async_computation.11 | async-start | bytes 1351680 | tf_op jit(solution)/shard_map/while/body/eval_jaxpr/all_gather | solution.py:130
  757.1 136.7 %reduce-scatter.10.cloned.1.call-start = ((), (), s32[]{:S(2)}) async-start(), calls=%async_computation.12 | async-start | bytes 2703360 | tf_op jit(solution)/shard_map/while/body/eval_jaxpr/reduce_scatter | solution.py:132
  849.1 76.3 %all-gather.12.cloned.1.call-start = ((), (), s32[]{:S(2)}) async-start(), calls=%async_computation.13 | async-start | bytes 1351680 | tf_op jit(solution)/shard_map/while/body/eval_jaxpr/all_gather | solution.py:139
  897.4 57.4 %all-gather.14.cloned.1.call-start = ((), (), s32[]{:S(2)}) async-start(), calls=%async_computation.14 | async-start | bytes 1351680 | tf_op jit(solution)/shard_map/while/body/eval_jaxpr/all_gather | solution.py:182
  897.5 15.8 collective-permute-start.1
  915.8 93.5 %reduce-scatter.12.cloned.1.call-start = ((), (), s32[]{:S(2)}) async-start(), calls=%async_computation.15 | async-start | bytes 2703360 | tf_op jit(solution)/shard_map/while/body/eval_jaxpr/reduce_scatter | solution.py:190
  1015.6 30.8 %all-to-all-start = ((bf16[4,176,768]{2,1,0:T(8,128)(2,1)}), bf16[4,176,768]{2,1,0:T(8,128)(2,1)}, u32[]{:S(2)}, u32[]{:S(2)}) async-start(bf16[4,176,768]{2,1,0:T(8,128)(2,1)} %stack.4), calls=%async_computation.4 | async-start | bytes 2162688 | tf_op jit(solution)/shard_map/while/body/eval_jaxpr/all_to_all | solution.py:15
  1019.9 153.6 %reduce-scatter.14.cloned.1.call-start = ((), (), s32[]{:S(2)}) async-start(), calls=%async_computation.16 | async-start | bytes 2703360 | tf_op jit(solution)/shard_map/while/body/eval_jaxpr/reduce_scatter | solution.py:207
  1142.0 34.3 %copy-start.106 = (f32[3,192]{1,0:T(4,128)}, f32[3,192]{1,0:T(4,128)S(1)}, u32[]{:S(2)}) copy-start(f32[3,192]{1,0:T(4,128)S(1)} %select_add_fusion.22) | copy-start | bytes 6916 | tf_op jit(solution)/shard_map/while
  1179.1 30.7 %all-gather.10.cloned.1.call-start = ((), (), s32[]{:S(2)}) async-start(), calls=%async_computation.11 | async-start | bytes 1351680 | tf_op jit(solution)/shard_map/while/body/eval_jaxpr/all_gather | solution.py:130
  1181.9 136.6 %reduce-scatter.10.cloned.1.call-start = ((), (), s32[]{:S(2)}) async-start(), calls=%async_computation.12 | async-start | bytes 2703360 | tf_op jit(solution)/shard_map/while/body/eval_jaxpr/reduce_scatter | solution.py:132
  1273.9 76.3 %all-gather.12.cloned.1.call-start = ((), (), s32[]{:S(2)}) async-start(), calls=%async_computation.13 | async-start | bytes 1351680 | tf_op jit(solution)/shard_map/while/body/eval_jaxpr/all_gather | solution.py:139
  1322.2 57.6 %all-gather.14.cloned.1.call-start = ((), (), s32[]{:S(2)}) async-start(), calls=%async_computation.14 | async-start | bytes 1351680 | tf_op jit(solution)/shard_map/while/body/eval_jaxpr/all_gather | solution.py:182
  1323.3 15.8 collective-permute-start.1
  1341.6 92.6 %reduce-scatter.12.cloned.1.call-start = ((), (), s32[]{:S(2)}) async-start(), calls=%async_computation.15 | async-start | bytes 2703360 | tf_op jit(solution)/shard_map/while/body/eval_jaxpr/reduce_scatter | solution.py:190
  1440.6 30.9 %all-to-all-start = ((bf16[4,176,768]{2,1,0:T(8,128)(2,1)}), bf16[4,176,768]{2,1,0:T(8,128)(2,1)}, u32[]{:S(2)}, u32[]{:S(2)}) async-start(bf16[4,176,768]{2,1,0:T(8,128)(2,1)} %stack.4), calls=%async_computation.4 | async-start | bytes 2162688 | tf_op jit(solution)/shard_map/while/body/eval_jaxpr/all_to_all | solution.py:15
  1444.8 153.7 %reduce-scatter.14.cloned.1.call-start = ((), (), s32[]{:S(2)}) async-start(), calls=%async_computation.16 | async-start | bytes 2703360 | tf_op jit(solution)/shard_map/while/body/eval_jaxpr/reduce_scatter | solution.py:207
  1604.1 30.8 %all-gather.10.cloned.1.call-start = ((), (), s32[]{:S(2)}) async-start(), calls=%async_computation.11 | async-start | bytes 1351680 | tf_op jit(solution)/shard_map/while/body/eval_jaxpr/all_gather | solution.py:130
  1606.8 136.6 %reduce-scatter.10.cloned.1.call-start = ((), (), s32[]{:S(2)}) async-start(), calls=%async_computation.12 | async-start | bytes 2703360 | tf_op jit(solution)/shard_map/while/body/eval_jaxpr/reduce_scatter | solution.py:132
  1698.9 76.3 %all-gather.12.cloned.1.call-start = ((), (), s32[]{:S(2)}) async-start(), calls=%async_computation.13 | async-start | bytes 1351680 | tf_op jit(solution)/shard_map/while/body/eval_jaxpr/all_gather | solution.py:139
  1747.1 57.6 %all-gather.14.cloned.1.call-start = ((), (), s32[]{:S(2)}) async-start(), calls=%async_computation.14 | async-start | bytes 1351680 | tf_op jit(solution)/shard_map/while/body/eval_jaxpr/all_gather | solution.py:182
  1748.3 15.8 collective-permute-start.1
  1766.6 92.6 %reduce-scatter.12.cloned.1.call-start = ((), (), s32[]{:S(2)}) async-start(), calls=%async_computation.15 | async-start | bytes 2703360 | tf_op jit(solution)/shard_map/while/body/eval_jaxpr/reduce_scatter | solution.py:190
  1865.5 30.9 %all-to-all-start = ((bf16[4,176,768]{2,1,0:T(8,128)(2,1)}), bf16[4,176,768]{2,1,0:T(8,128)(2,1)}, u32[]{:S(2)}, u32[]{:S(2)}) async-start(bf16[4,176,768]{2,1,0:T(8,128)(2,1)} %stack.4), calls=%async_computation.4 | async-start | bytes 2162688 | tf_op jit(solution)/shard_map/while/body/eval_jaxpr/all_to_all | solution.py:15
  1869.8 153.7 %reduce-scatter.14.cloned.1.call-start = ((), (), s32[]{:S(2)}) async-start(), calls=%async_computation.16 | async-start | bytes 2703360 | tf_op jit(solution)/shard_map/while/body/eval_jaxpr/reduce_scatter | solution.py:207
  2030.8 197.2 %all-reduce.39.cloned.1.call-start = ((), (), s32[]{:S(2)}) async-start(), calls=%async_computation.6 | async-start | bytes 21233664 | tf_op jit(solution)/shard_map/psum | solution.py:355
  2037.5 34.6 %copy-start.123 = (f32[2,192]{1,0:T(2,128)S(1)}, f32[2,192]{1,0:T(2,128)}, u32[]{:S(2)}) copy-start(f32[2,192]{1,0:T(2,128)} %get-tuple-element.559) | copy-start | bytes 4612
  (383 other events, 2625.5 us)
Sparse Core Ops, SparseCore 0:
  67.3 30.7 all-gather.5
  157.3 44.4 reduce-scatter.5
  204.2 27.8 all-gather.7
  238.8 44.4 reduce-scatter.7
  302.6 29.0 all-gather.5
  390.9 44.4 reduce-scatter.5
  437.8 27.8 all-gather.7
  472.4 44.4 reduce-scatter.7
  536.3 29.0 all-gather.5
  624.6 44.4 reduce-scatter.5
  671.5 27.8 all-gather.7
  706.1 44.4 reduce-scatter.7
  757.2 27.8 all-gather.9
  849.3 44.4 reduce-scatter.9
  897.5 27.8 all-gather.11
  926.8 27.9 all-gather.13
  964.8 44.4 reduce-scatter.11
  1129.5 43.9 reduce-scatter.13
  1182.0 27.8 all-gather.9
  1274.1 44.4 reduce-scatter.9
  1322.3 27.8 all-gather.11
  1351.8 27.9 all-gather.13
  1389.7 44.4 reduce-scatter.11
  1554.5 43.9 reduce-scatter.13
  1607.0 27.8 all-gather.9
  1699.0 44.4 reduce-scatter.9
  1747.3 27.8 all-gather.11
  1776.7 27.9 all-gather.13
  1814.7 44.4 reduce-scatter.11
  1979.4 43.9 reduce-scatter.13
Sparse Core Ops, SparseCore 1:
  2037.6 190.3 all-reduce.38
